TPU v7x, 256 devices: a whole 4x4x8 slice. The times are simulated.
256 devices in a mesh: bus: 32 (over x, z), case: 8 (over y, core).
Axes of the slice: x: 4, y: 4, z: 8, core: 2. Of those that a mesh axis runs over, the one named last changes fastest.
Arguments:
- z_columns: float32 [32768, 1024], P('bus')
- resident_bus: int32 [1024], replicated, may hold values from 0 to 32767, as said below
- fault_col: int32 [4096], P('case'), may hold values from 0 to 1023
- switch_cols: int32 [4096, 2], P('case'), may hold values from 0 to 1023, as said below
- tie_x: float32 [4096], P('case'), may hold values from 0.5 to 2
- fault_z: float32 [4096], P('case'), may hold values from 0.5 to 2
- boundary_send: int32 [32, 2, 128], replicated, may hold values from 0 to 1023, as said below
- branch_ends: int32 [49152, 2], P('bus'), may hold values from 0 to 1279, as said below
- branch_x: float32 [49152], P('bus'), may hold values from 0.01 to 0.05
- pickup: float32 [49152], P('bus'), may hold values from 0.2 to 1.5
- tds: float32 [49152], P('bus'), may hold values from 0.05 to 0.5
- curve: int32 [49152], P('bus'), may hold values from 0 to 2
Outputs:
- voltage: float32 [32768, 4096], P('bus', 'case')
- relay_rate: float32 [49152, 4096], P('bus', 'case')
- worst_rate: float32 [49152], P('bus')
Inputs may be any that keep to these rules, and one draw needn't show every extreme that they name: `resident_bus`: distinct bus ids. `switch_cols`: the two columns of a case differ. `boundary_send`: rows sent to the lower block lie among the first 256 rows, rows sent to the upper block among the last 256; each block's live slots come first and hold distinct rows, padding repeats the first slot's row; the first block sends nothing down and the last nothing up; some block fills all 128 slots. `branch_ends`: a to slot of 1024 or more points at a live slot of the neighbour's block; the first block never uses the lower slots, the last never the upper ones; a local to row differs from the from row.
All inputs are finite; a program needn't handle non-finite values.
Results may differ from a plain program's by a relative error of at most 0.000049.
Values sent between devices are 32-bit elements; how exact they have to be, the bound alone decides.
A program may use at most 64 MiB of HBM per device.

v0:
```python
import jax
import jax.numpy as jnp
from jax import lax
from jax.sharding import PartitionSpec as P


def shifted(value, axis, by):
    size = lax.axis_size(axis)
    pairs = [(i, i + by) for i in range(size) if 0 <= i + by < size]
    return lax.ppermute(value, axis, pairs)


def relay_of(currents, pickup, tds, curve):
    factor = jnp.where(curve == 0, 0.14, jnp.where(curve == 1, 13.5, 80.0)).astype(jnp.float32)
    exponent = jnp.where(curve == 0, 0.02, jnp.where(curve == 1, 1.0, 2.0)).astype(jnp.float32)
    scaled = currents / pickup[:, None]
    powered = jnp.exp(0.5 * exponent[:, None] * jnp.log(scaled * scaled + 0.0001))
    return jnp.maximum(powered - 1.0, 0.0) / (factor * tds)[:, None]


def per_device(
    z_columns,
    resident_bus,
    fault_col,
    switch_cols,
    tie_x,
    fault_z,
    boundary_send,
    branch_ends,
    branch_x,
    pickup,
    tds,
    curve,
):
    rows_dev = z_columns.shape[0]
    my_index = lax.axis_index("bus")
    fault_cols = jnp.take(z_columns, fault_col, axis=1)
    branch_diff = jnp.take(z_columns, switch_cols[:, 0], axis=1) - jnp.take(
        z_columns, switch_cols[:, 1], axis=1
    )
    offset = my_index * rows_dev
    row_a = jnp.take(resident_bus, switch_cols[:, 0]) - offset
    row_b = jnp.take(resident_bus, switch_cols[:, 1]) - offset
    row_f = jnp.take(resident_bus, fault_col) - offset
    row_ids = lax.broadcasted_iota(jnp.int32, (rows_dev, 1), 0)

    def pick_rows(column, wanted):
        return jnp.sum(jnp.where(row_ids == wanted[None, :], column, 0.0), axis=0)

    partial_value = jnp.stack(
        [
            pick_rows(branch_diff, row_a) - pick_rows(branch_diff, row_b),
            pick_rows(branch_diff, row_f),
            pick_rows(fault_cols, row_f),
        ]
    )
    own_lists = lax.dynamic_index_in_dim(boundary_send, my_index, 0, keepdims=False)
    entry_sums = lax.psum(partial_value, "bus")
    weight_ratio = entry_sums[1] / (tie_x + entry_sums[0])
    self_z = entry_sums[2] - entry_sums[1] * weight_ratio
    fault_amps = 1.0 / (self_z + fault_z)
    voltage = 1.0 - (fault_cols - branch_diff * weight_ratio[None, :]) * fault_amps[None, :]
    fields = voltage[None]
    going_down = jnp.take(fields, own_lists[0], axis=1)
    going_up = jnp.take(fields, own_lists[1], axis=1)
    from_lower = shifted(going_up, "bus", 1)
    from_upper = shifted(going_down, "bus", -1)
    extended = jnp.concatenate([fields, from_lower, from_upper], axis=1)[0]
    drops = jnp.take(extended, branch_ends[:, 0], axis=0) - jnp.take(
        extended, branch_ends[:, 1], axis=0
    )
    currents = drops / branch_x[:, None]
    relay_rate = relay_of(currents, pickup, tds, curve)
    worst_rate = lax.pmax(jnp.max(relay_rate, axis=1), "case")
    return (voltage, relay_rate, worst_rate)


def solution(mesh):
    in_specs = (
        P("bus", None),
        P(),
        P("case"),
        P("case", None),
        P("case"),
        P("case"),
        P(),
        P("bus", None),
        P("bus"),
        P("bus"),
        P("bus"),
        P("bus"),
    )
    out_specs = (P("bus", "case"), P("bus", "case"), P("bus"))
    return jax.shard_map(
        per_device, mesh=mesh, in_specs=in_specs, out_specs=out_specs, check_vma=False
    )
```

profile of v0, /device:TPU:1, one launch (start us, length us, event | category | flops | bytes accessed | tf_op | source)
XLA Modules:
  0.0 166.8 jit_solution(13267739268833994264)
XLA Ops:
  0.6 0.0 copy-start
  0.6 0.0 copy-start.1
  0.7 0.8 fusion.11
  1.5 3.4 %gather_fusion.4 = s32[512]{0:T(512)S(1)} fusion(s32[1024]{0:T(1024)} %param.21, s32[1024]{0:T(1024)S(1)} %pad_clamp_fusion.4), kind=kCustom, calls=%fused_computation.6.clone | custom fusion | bytes 6144 | tf_op jit(solution)/shard_map/jit(_take)/gather | solution.py:43
  4.8 0.0 copy-done.1
  4.8 2.3 %gather_fusion.3 = s32[512]{0:T(512)S(1)} fusion(s32[1024]{0:T(1024)S(1)} %copy-done.1, s32[1024]{0:T(1024)S(1)} %pad_clamp_fusion.5), kind=kCustom, calls=%fused_computation.1.clone | custom fusion | bytes 6144 | tf_op jit(solution)/shard_map/jit(_take)/gather | solution.py:42
  7.1 5.4 %copy.25 = f32[1024,1024]{0,1:T(8,128)} copy(f32[1024,1024]{1,0:T(8,128)} %param.20) | data formatting | bytes 8388608 | tf_op args[0]
  12.5 5.8 %gather_fusion.1 = f32[512,1024]{1,0:T(8,128)} fusion(f32[1024,1024]{0,1:T(8,128)} %copy.25, s32[1024]{0:T(1024)S(1)} %pad_clamp_fusion.5), kind=kCustom, calls=%fused_computation.4.clone | custom fusion | bytes 4196352 | tf_op jit(solution)/shard_map/jit(_take)/gather | solution.py:38
  18.3 0.0 copy-start.6
  18.3 5.8 %gather_fusion.2 = f32[512,1024]{1,0:T(8,128)} fusion(f32[1024,1024]{0,1:T(8,128)} %copy.25, s32[1024]{0:T(1024)S(1)} %pad_clamp_fusion.4), kind=kCustom, calls=%fused_computation.5.clone | custom fusion | bytes 4196352 | tf_op jit(solution)/shard_map/jit(_take)/gather | solution.py:38
  24.1 0.0 copy-done.6
  24.1 2.3 %gather_fusion.5 = s32[512]{0:T(512)S(1)} fusion(s32[1024]{0:T(1024)S(1)} %copy-done.1, s32[1024]{0:T(1024)S(1)} %pad_clamp_fusion.6), kind=kCustom, calls=%fused_computation.7.clone | custom fusion | bytes 6144 | tf_op jit(solution)/shard_map/jit(_take)/gather | solution.py:44
  26.4 5.0 %gather_fusion = f32[512,1024]{1,0:T(8,128)S(1)} fusion(f32[1024,1024]{0,1:T(8,128)} %copy.25, s32[1024]{0:T(1024)S(1)} %pad_clamp_fusion.6), kind=kCustom, calls=%fused_computation.clone | custom fusion | bytes 4196352 | tf_op jit(solution)/shard_map/jit(_take)/gather | solution.py:37
  31.5 0.0 copy-start.9
  31.5 0.0 copy-start.10
  31.5 4.2 %select_reduce_fusion.1 = (f32[512]{0:T(512)S(1)}, f32[512]{0:T(512)S(1)}, f32[512]{0:T(512)S(1)}, f32[512]{0:T(512)S(1)}, f32[1024,512]{0,1:T(8,128)}) fusion(s32[512]{0:T(512)S(1)} %get-tuple-element.44, s32[512]{0:T(512)S(1)} %get-tuple-element.33, s32[512]{0:T(512)S(1)} %get-tuple-element.31, f32[512,1024]{1,0:T(8,128)S(1)} %gather_fusion, ...), kind=kLoop, calls=%fused_computation.27 | loop fusion | flops 7862272 | bytes 8404480 | tf_op jit(solution)/shard_map/reduce_sum | solution.py:48
  35.7 65.3 %psum.7 = f32[3,512]{1,0:T(4,128)S(1)} all-reduce(f32[3,512]{1,0:T(4,128)S(1)} %pad_maximum_fusion), channel_id=1, replica_groups=mesh['bus'=32,'case'=8] {'bus'}, use_global_device_ids=true, to_apply=%region_4.7 | all-reduce | flops 1536 | bytes 12288 | tf_op jit(solution)/shard_map/psum | solution.py:58
  101.1 0.0 copy-done.9
  101.1 0.0 copy-done.10
  101.1 3.4 %fusion.8 = f32[1024,512]{0,1:T(8,128)} fusion(f32[1024,512]{0,1:T(8,128)} %get-tuple-element.30, f32[512,1024]{1,0:T(8,128)S(1)} %gather_fusion, f32[512]{0:T(512)S(1)} %get-tuple-element.28, f32[512]{0:T(512)S(1)} %get-tuple-element.29, pred[512]{0:T(512)(128)(4,1)S(1)} %get-tuple-element.34), kind=kLoop, calls=%fused_computation.24 | loop fusion | flops 2621440 | bytes 6296064 | tf_op jit(solution)/shard_map/sub | solution.py:62
  104.5 1.9 %copy.34 = f32[1024,512]{1,0:T(8,128)S(1)} copy(f32[1024,512]{0,1:T(8,128)} %fusion.8) | data formatting | bytes 4194304
  106.4 0.0 copy-start.2
  106.5 0.0 copy-done
  106.5 0.8 gather_fusion.6
  107.3 0.1 copy.29
  107.4 0.0 copy-start.3
  107.4 0.0 copy-start.7
  107.4 0.0 copy-start.4
  107.4 0.0 copy-start.5
  107.5 0.0 copy-start.8
  107.5 1.3 collective-permute-start
  108.8 0.8 gather_fusion.7
  109.6 0.0 copy-done.2
  109.6 0.1 copy.31
  109.7 1.3 collective-permute-start.1
  111.0 0.0 copy-done.3
  111.1 0.0 copy-done.7
  111.2 0.0 copy-done.4
  111.2 0.0 copy-done.5
  111.2 0.0 copy-done.8
  111.2 0.9 collective-permute-done
  112.2 4.7 %collective-permute-done.1 = f32[1,128,512]{1,2,0:T(8,128)S(1)} collective-permute-done((f32[1,128,512]{1,2,0:T(8,128)S(1)}, f32[1,128,512]{1,2,0:T(8,128)S(1)}, u32[]{:S(2)}, u32[]{:S(2)}) %collective-permute-start.1) | collective-permute-done | bytes 262176 | tf_op jit(solution)/shard_map/ppermute | solution.py:10
  116.9 3.3 %maximum_bitcast_fusion = f32[1280,512]{0,1:T(8,128)} fusion(f32[1,128,512]{1,2,0:T(8,128)S(1)} %collective-permute-done.1, f32[1,128,512]{1,2,0:T(8,128)S(1)} %collective-permute-done, f32[1,1024,512]{1,2,0:T(8,128)} %bitcast.36), kind=kLoop, calls=%fused_computation.18 | loop fusion | flops 1310720 | bytes 5242880 | tf_op jit(solution)/shard_map/squeeze | solution.py:68
  120.2 2.1 %copy.32 = f32[1280,512]{1,0:T(8,128)S(1)} copy(f32[1280,512]{0,1:T(8,128)} %maximum_bitcast_fusion) | data formatting | bytes 5242880 | tf_op jit(solution)/shard_map/squeeze | solution.py:68
  122.3 5.0 %gather_fusion.8 = f32[1536,512]{1,0:T(8,128)} fusion(f32[1280,512]{1,0:T(8,128)S(1)} %copy.32, s32[2048]{0:T(1024)S(1)} %pad_clamp_fusion.1), kind=kCustom, calls=%fused_computation.3.clone | custom fusion | bytes 6297600 | tf_op jit(solution)/shard_map/jit(_take)/gather | solution.py:69
  127.3 4.9 %gather_fusion.9 = f32[1536,512]{1,0:T(8,128)} fusion(f32[1280,512]{1,0:T(8,128)S(1)} %copy.32, s32[2048]{0:T(1024)S(1)} %pad_clamp_fusion), kind=kCustom, calls=%fused_computation.9.clone | custom fusion | bytes 6297600 | tf_op jit(solution)/shard_map/jit(_take)/gather | solution.py:69
  132.2 5.9 %fusion.9 = (f32[1536]{0:T(1024)S(1)}, f32[1536,512]{1,0:T(8,128)}) fusion(f32[1536]{0:T(1024)S(1)} %select_multiply_fusion, f32[1536]{0:T(1024)S(1)} %multiply.4, f32[1536,512]{1,0:T(8,128)} %gather_fusion.9, pred[1536]{0:T(1024)(128)(4,1)S(1)} %get-tuple-element.48, f32[1536,512]{1,0:T(8,128)} %gather_fusion.8, pred[1536]{0:T(1024)(128)(4,1)S(1)} %get-tuple-element.49, ...), kind=kLoop, calls=%fused_computation.67 | loop fusion | flops 8649216 | bytes 9464832 | tf_op jit(solution)/shard_map/reduce_max | solution.py:74
  138.1 28.7 %pmax.7 = f32[1536]{0:T(1024)} all-reduce(f32[1536]{0:T(1024)S(1)} %get-tuple-element.19), channel_id=1, replica_groups=mesh['bus'=32,'case'=8] {'case'}, use_global_device_ids=true, to_apply=%region_6.11 | all-reduce | flops 1536 | bytes 12288 | tf_op jit(solution)/shard_map/pmax | solution.py:74
  (26 shorter events, 0.3 us)
Async XLA Ops:
  0.6 105.8 %copy-start = (s32[32,2,128]{2,1,0:T(2,128)S(1)}, s32[32,2,128]{2,1,0:T(2,128)}, u32[]{:S(2)}) copy-start(s32[32,2,128]{2,1,0:T(2,128)} %param.26) | copy-start | bytes 98308
  0.6 4.2 %copy-start.1 = (s32[1024]{0:T(1024)S(1)}, s32[1024]{0:T(1024)}, u32[]{:S(2)}) copy-start(s32[1024]{0:T(1024)} %param.21) | copy-start | bytes 12292
  18.3 5.8 %copy-start.6 = (s32[512]{0:T(512)S(1)}, s32[512]{0:T(512)}, u32[]{:S(2)}) copy-start(s32[512]{0:T(512)} %param.22) | copy-start | bytes 6148
  31.5 69.6 %copy-start.9 = (f32[512]{0:T(512)S(1)}, f32[512]{0:T(512)}, u32[]{:S(2)}) copy-start(f32[512]{0:T(512)} %param.25) | copy-start | bytes 6148
  31.5 69.6 %copy-start.10 = (f32[512]{0:T(512)S(1)}, f32[512]{0:T(512)}, u32[]{:S(2)}) copy-start(f32[512]{0:T(512)} %param.24) | copy-start | bytes 6148
  106.4 3.1 %copy-start.2 = (f32[1024,512]{1,0:T(8,128)}, f32[1024,512]{1,0:T(8,128)S(1)}, u32[]{:S(2)}) copy-start(f32[1024,512]{1,0:T(8,128)S(1)} %copy.34) | copy-start | bytes 6291460
  107.4 3.6 %copy-start.3 = (s32[1536,2]{0,1:T(2,128)S(1)}, s32[1536,2]{0,1:T(2,128)}, u32[]{:S(2)}) copy-start(s32[1536,2]{0,1:T(2,128)} %param.27) | copy-start | bytes 36868
  107.4 3.7 %copy-start.7 = (s32[1536]{0:T(1024)S(1)}, s32[1536]{0:T(1024)}, u32[]{:S(2)}) copy-start(s32[1536]{0:T(1024)} %param.31) | copy-start | bytes 18436
  107.4 3.8 %copy-start.4 = (f32[1536]{0:T(1024)S(1)}, f32[1536]{0:T(1024)}, u32[]{:S(2)}) copy-start(f32[1536]{0:T(1024)} %param.28) | copy-start | bytes 18436
  107.4 3.8 %copy-start.5 = (f32[1536]{0:T(1024)S(1)}, f32[1536]{0:T(1024)}, u32[]{:S(2)}) copy-start(f32[1536]{0:T(1024)} %param.29) | copy-start | bytes 18436
  107.5 3.8 %copy-start.8 = (f32[1536]{0:T(1024)S(1)}, f32[1536]{0:T(1024)}, u32[]{:S(2)}) copy-start(f32[1536]{0:T(1024)} %param.30) | copy-start | bytes 18436
  107.5 4.7 %collective-permute-start = (f32[1,128,512]{1,2,0:T(8,128)S(1)}, f32[1,128,512]{1,2,0:T(8,128)S(1)}, u32[]{:S(2)}, u32[]{:S(2)}) collective-permute-start(f32[1,128,512]{1,2,0:T(8,128)S(1)} %bitcast_select_fusion.2), channel_id=1, source_target_pairs={{0,8},{8,16},{16,24},{24,32},{32,40},{40,48},{48,56},{56,64},{64,7... | collective-permute-start | bytes 786440 | tf_op jit(solution)/shard_map/ppermute | solution.py:10
  109.7 7.1 %collective-permute-start.1 = (f32[1,128,512]{1,2,0:T(8,128)S(1)}, f32[1,128,512]{1,2,0:T(8,128)S(1)}, u32[]{:S(2)}, u32[]{:S(2)}) collective-permute-start(f32[1,128,512]{1,2,0:T(8,128)S(1)} %bitcast_select_fusion.1), channel_id=1, source_target_pairs={{8,0},{16,8},{24,16},{32,24},{40,32},{48,40},{56,48},{64,56},{72,6... | collective-permute-start | bytes 786440 | tf_op jit(solution)/shard_map/ppermute | solution.py:10
where the time goes:
time: 167 us
  blocking collectives  94.1 us (56%)
  local copies, waits for them, and re-layouts  46.5 us (28%)
  other arithmetic  17 us (10%)
  waiting for transfers between devices  5.62 us (3%)
  starting transfers between devices  2.6 us (2%)
    psum x1, blocking collectives, per_device(): entry_sums = lax.psum(partial_value, 'bus')  65.3 us
    pmax x1, blocking collectives, per_device(): worst_rate = lax.pmax(jnp.max(relay_rate, axis=1), 'case')  28.7 us
    unnamed x24, local copies, waits for them, and re-layouts  7.35 us
    reduce_max x1, other arithmetic, per_device(): worst_rate = lax.pmax(jnp.max(relay_rate, axis=1), 'case')  5.9 us
    gather x1, local copies, waits for them, and re-layouts, per_device(): jnp.take(z_columns, switch_cols[:, 1], axis=1)  5.8 us
    gather x1, local copies, waits for them, and re-layouts, per_device(): jnp.take(z_columns, switch_cols[:, 0], axis=1)  5.78 us
    ppermute x2, waiting for transfers between devices, shifted(): return lax.ppermute(value, axis, pairs)  5.62 us
    gather x1, local copies, waits for them, and re-layouts, per_device(): fault_cols = jnp.take(z_columns, fault_col, axis=1)  5.01 us
  transfers between devices with their start and end apart: 2, of which 2 were waited for; matrix products, arithmetic and copies ran while one was open for 1% of the time, Pallas kernels for 0%

commit v1 on v0

--- a/solution.py
+++ b/solution.py
@@ -55,7 +55,7 @@
         ]
     )
     own_lists = lax.dynamic_index_in_dim(boundary_send, my_index, 0, keepdims=False)
-    entry_sums = lax.psum(partial_value, "bus")
+    entry_sums = jnp.sum(lax.all_gather(partial_value, "bus"), axis=0)
     weight_ratio = entry_sums[1] / (tie_x + entry_sums[0])
     self_z = entry_sums[2] - entry_sums[1] * weight_ratio
     fault_amps = 1.0 / (self_z + fault_z)

time: 167 us -> 143 us (0.86)
  blocking collectives: 94.1 us -> 68.1 us
    psum x1 -> x0, blocking collectives: 65.3 us -> none  [per_device(): entry_sums = lax.psum(partial_value, 'bus')]
    all_gather x0 -> x1, blocking collectives: none -> 40.8 us  [per_device(): entry_sums = jnp.sum(lax.all_gather(partial_value, 'bus'), axis=0)]
where the time goes in v1:
time: 143 us; the launch traced here: 142 us
  blocking collectives  68.1 us (48%)
  local copies, waits for them, and re-layouts  46.5 us (33%)
  other arithmetic  17.1 us (12%)
  waiting for transfers between devices  5.62 us (4%)
  starting transfers between devices  3.84 us (3%)
    all_gather x1, blocking collectives, per_device(): entry_sums = jnp.sum(lax.all_gather(partial_value, 'bus'), axis=0)  40.8 us
    pmax x1, blocking collectives, per_device(): worst_rate = lax.pmax(jnp.max(relay_rate, axis=1), 'case')  27.3 us
    unnamed x24, local copies, waits for them, and re-layouts  7.35 us
    reduce_max x1, other arithmetic, per_device(): worst_rate = lax.pmax(jnp.max(relay_rate, axis=1), 'case')  5.9 us
    gather x1, local copies, waits for them, and re-layouts, per_device(): jnp.take(z_columns, switch_cols[:, 1], axis=1)  5.8 us
    gather x1, local copies, waits for them, and re-layouts, per_device(): jnp.take(z_columns, switch_cols[:, 0], axis=1)  5.78 us
    ppermute x2, waiting for transfers between devices, shifted(): return lax.ppermute(value, axis, pairs)  5.62 us
    gather x1, local copies, waits for them, and re-layouts, per_device(): fault_cols = jnp.take(z_columns, fault_col, axis=1)  5.01 us
  transfers between devices with their start and end apart: 2, of which 2 were waited for; matrix products, arithmetic and copies ran while one was open for 1% of the time, Pallas kernels for 0%

profile of v1, /device:TPU:1, one launch (start us, length us, event | category | flops | bytes accessed | tf_op | source)
XLA Modules:
  0.0 142.2 jit_solution(4963782477146650624)
XLA Ops:
  0.6 0.0 copy-start
  0.6 0.0 copy-start.1
  0.7 0.8 fusion.11
  1.5 3.4 %gather_fusion.4 = s32[512]{0:T(512)S(1)} fusion(s32[1024]{0:T(1024)} %param.21, s32[1024]{0:T(1024)S(1)} %pad_clamp_fusion.4), kind=kCustom, calls=%fused_computation.6.clone | custom fusion | bytes 6144 | tf_op jit(solution)/shard_map/jit(_take)/gather | solution.py:43
  4.8 0.0 copy-done.1
  4.8 2.3 %gather_fusion.3 = s32[512]{0:T(512)S(1)} fusion(s32[1024]{0:T(1024)S(1)} %copy-done.1, s32[1024]{0:T(1024)S(1)} %pad_clamp_fusion.5), kind=kCustom, calls=%fused_computation.1.clone | custom fusion | bytes 6144 | tf_op jit(solution)/shard_map/jit(_take)/gather | solution.py:42
  7.1 5.4 %copy.35 = f32[1024,1024]{0,1:T(8,128)} copy(f32[1024,1024]{1,0:T(8,128)} %param.20) | data formatting | bytes 8388608 | tf_op args[0]
  12.5 5.8 %gather_fusion.1 = f32[512,1024]{1,0:T(8,128)} fusion(f32[1024,1024]{0,1:T(8,128)} %copy.35, s32[1024]{0:T(1024)S(1)} %pad_clamp_fusion.5), kind=kCustom, calls=%fused_computation.4.clone | custom fusion | bytes 4196352 | tf_op jit(solution)/shard_map/jit(_take)/gather | solution.py:38
  18.3 0.0 copy-start.6
  18.3 5.8 %gather_fusion.2 = f32[512,1024]{1,0:T(8,128)} fusion(f32[1024,1024]{0,1:T(8,128)} %copy.35, s32[1024]{0:T(1024)S(1)} %pad_clamp_fusion.4), kind=kCustom, calls=%fused_computation.5.clone | custom fusion | bytes 4196352 | tf_op jit(solution)/shard_map/jit(_take)/gather | solution.py:38
  24.1 0.0 copy-done.6
  24.1 2.3 %gather_fusion.5 = s32[512]{0:T(512)S(1)} fusion(s32[1024]{0:T(1024)S(1)} %copy-done.1, s32[1024]{0:T(1024)S(1)} %pad_clamp_fusion.6), kind=kCustom, calls=%fused_computation.7.clone | custom fusion | bytes 6144 | tf_op jit(solution)/shard_map/jit(_take)/gather | solution.py:44
  26.4 5.0 %gather_fusion = f32[512,1024]{1,0:T(8,128)S(1)} fusion(f32[1024,1024]{0,1:T(8,128)} %copy.35, s32[1024]{0:T(1024)S(1)} %pad_clamp_fusion.6), kind=kCustom, calls=%fused_computation.clone | custom fusion | bytes 4196352 | tf_op jit(solution)/shard_map/jit(_take)/gather | solution.py:37
  31.5 0.0 copy-start.9
  31.5 0.0 copy-start.10
  31.5 4.2 %select_reduce_fusion.1 = (f32[512]{0:T(512)S(1)}, f32[512]{0:T(512)S(1)}, f32[512]{0:T(512)S(1)}, f32[512]{0:T(512)S(1)}, f32[1024,512]{0,1:T(8,128)}) fusion(s32[512]{0:T(512)S(1)} %get-tuple-element.47, s32[512]{0:T(512)S(1)} %get-tuple-element.36, s32[512]{0:T(512)S(1)} %get-tuple-element.34, f32[512,1024]{1,0:T(8,128)S(1)} %gather_fusion, ...), kind=kLoop, calls=%fused_computation.27 | loop fusion | flops 7862272 | bytes 8404480 | tf_op jit(solution)/shard_map/reduce_sum | solution.py:48
  35.7 40.8 %all-gather.1 = f32[32,3,512]{2,1,0:T(4,128)S(1)} all-gather(f32[1,3,512]{2,1,0:T(4,128)S(1)} %maximum_bitcast_fusion.1), channel_id=2, replica_groups=mesh['bus'=32,'case'=8] {'bus'}, dimensions={0}, use_global_device_ids=true | all-gather | bytes 202752 | tf_op jit(solution)/shard_map/all_gather | solution.py:58
  76.6 0.1 reduce_sum.49
  76.6 0.0 copy-done.9
  76.7 0.0 copy-done.10
  76.7 3.4 %fusion.8 = f32[1024,512]{0,1:T(8,128)} fusion(f32[1024,512]{0,1:T(8,128)} %get-tuple-element.33, f32[512,1024]{1,0:T(8,128)S(1)} %gather_fusion, f32[512]{0:T(512)S(1)} %get-tuple-element.31, f32[512]{0:T(512)S(1)} %get-tuple-element.32, pred[512]{0:T(512)(128)(4,1)S(1)} %get-tuple-element.37), kind=kLoop, calls=%fused_computation.24 | loop fusion | flops 2621440 | bytes 6296064 | tf_op jit(solution)/shard_map/sub | solution.py:62
  80.1 1.9 %copy.44 = f32[1024,512]{1,0:T(8,128)S(1)} copy(f32[1024,512]{0,1:T(8,128)} %fusion.8) | data formatting | bytes 4194304
  82.0 0.0 copy-start.2
  82.0 0.0 copy-done
  82.1 0.8 gather_fusion.6
  82.8 0.1 copy.39
  83.0 0.0 copy-start.3
  83.0 0.0 copy-start.7
  83.0 0.0 copy-start.4
  83.0 0.0 copy-start.5
  83.0 0.0 copy-start.8
  83.1 2.5 %collective-permute-start = (f32[1,128,512]{1,2,0:T(8,128)S(1)}, f32[1,128,512]{1,2,0:T(8,128)S(1)}, u32[]{:S(2)}, u32[]{:S(2)}) collective-permute-start(f32[1,128,512]{1,2,0:T(8,128)S(1)} %bitcast_select_fusion.2), channel_id=1, source_target_pairs={{0,8},{8,16},{16,24},{24,32},{32,40},{40,48},{48,56},{56,64},{64,7... | collective-permute-start | bytes 786440 | tf_op jit(solution)/shard_map/ppermute | solution.py:10
  85.6 0.8 gather_fusion.7
  86.4 0.0 copy-done.2
  86.4 0.1 copy.41
  86.6 1.3 collective-permute-start.1
  87.9 0.0 copy-done.3
  88.0 0.0 copy-done.7
  88.0 0.0 copy-done.4
  88.0 0.0 copy-done.5
  88.0 0.0 copy-done.8
  88.1 0.9 collective-permute-done
  89.0 4.7 %collective-permute-done.1 = f32[1,128,512]{1,2,0:T(8,128)S(1)} collective-permute-done((f32[1,128,512]{1,2,0:T(8,128)S(1)}, f32[1,128,512]{1,2,0:T(8,128)S(1)}, u32[]{:S(2)}, u32[]{:S(2)}) %collective-permute-start.1) | collective-permute-done | bytes 262176 | tf_op jit(solution)/shard_map/ppermute | solution.py:10
  93.7 3.3 %maximum_bitcast_fusion = f32[1280,512]{0,1:T(8,128)} fusion(f32[1,128,512]{1,2,0:T(8,128)S(1)} %collective-permute-done.1, f32[1,128,512]{1,2,0:T(8,128)S(1)} %collective-permute-done, f32[1,1024,512]{1,2,0:T(8,128)} %bitcast.38), kind=kLoop, calls=%fused_computation.18 | loop fusion | flops 1310720 | bytes 5242880 | tf_op jit(solution)/shard_map/squeeze | solution.py:68
  97.0 2.1 %copy.42 = f32[1280,512]{1,0:T(8,128)S(1)} copy(f32[1280,512]{0,1:T(8,128)} %maximum_bitcast_fusion) | data formatting | bytes 5242880 | tf_op jit(solution)/shard_map/squeeze | solution.py:68
  99.1 5.0 %gather_fusion.8 = f32[1536,512]{1,0:T(8,128)} fusion(f32[1280,512]{1,0:T(8,128)S(1)} %copy.42, s32[2048]{0:T(1024)S(1)} %pad_clamp_fusion.1), kind=kCustom, calls=%fused_computation.3.clone | custom fusion | bytes 6297600 | tf_op jit(solution)/shard_map/jit(_take)/gather | solution.py:69
  104.1 4.9 %gather_fusion.9 = f32[1536,512]{1,0:T(8,128)} fusion(f32[1280,512]{1,0:T(8,128)S(1)} %copy.42, s32[2048]{0:T(1024)S(1)} %pad_clamp_fusion), kind=kCustom, calls=%fused_computation.9.clone | custom fusion | bytes 6297600 | tf_op jit(solution)/shard_map/jit(_take)/gather | solution.py:69
  109.0 5.9 %fusion.9 = (f32[1536]{0:T(1024)S(1)}, f32[1536,512]{1,0:T(8,128)}) fusion(f32[1536]{0:T(1024)S(1)} %select_multiply_fusion, f32[1536]{0:T(1024)S(1)} %multiply.4, f32[1536,512]{1,0:T(8,128)} %gather_fusion.9, pred[1536]{0:T(1024)(128)(4,1)S(1)} %get-tuple-element.51, f32[1536,512]{1,0:T(8,128)} %gather_fusion.8, pred[1536]{0:T(1024)(128)(4,1)S(1)} %get-tuple-element.52, ...), kind=kLoop, calls=%fused_computation.67 | loop fusion | flops 8649216 | bytes 9464832 | tf_op jit(solution)/shard_map/reduce_max | solution.py:74
  114.9 27.3 %pmax.7 = f32[1536]{0:T(1024)} all-reduce(f32[1536]{0:T(1024)S(1)} %get-tuple-element.22), channel_id=1, replica_groups=mesh['bus'=32,'case'=8] {'case'}, use_global_device_ids=true, to_apply=%region_6.11 | all-reduce | flops 1536 | bytes 12288 | tf_op jit(solution)/shard_map/pmax | solution.py:74
  (26 shorter events, 0.3 us)
Async XLA Ops:
  0.6 81.4 %copy-start = (s32[32,2,128]{2,1,0:T(2,128)S(1)}, s32[32,2,128]{2,1,0:T(2,128)}, u32[]{:S(2)}) copy-start(s32[32,2,128]{2,1,0:T(2,128)} %param.26) | copy-start | bytes 98308
  0.6 4.2 %copy-start.1 = (s32[1024]{0:T(1024)S(1)}, s32[1024]{0:T(1024)}, u32[]{:S(2)}) copy-start(s32[1024]{0:T(1024)} %param.21) | copy-start | bytes 12292
  18.3 5.8 %copy-start.6 = (s32[512]{0:T(512)S(1)}, s32[512]{0:T(512)}, u32[]{:S(2)}) copy-start(s32[512]{0:T(512)} %param.22) | copy-start | bytes 6148
  31.5 45.2 %copy-start.9 = (f32[512]{0:T(512)S(1)}, f32[512]{0:T(512)}, u32[]{:S(2)}) copy-start(f32[512]{0:T(512)} %param.25) | copy-start | bytes 6148
  31.5 45.2 %copy-start.10 = (f32[512]{0:T(512)S(1)}, f32[512]{0:T(512)}, u32[]{:S(2)}) copy-start(f32[512]{0:T(512)} %param.24) | copy-start | bytes 6148
  82.0 4.4 %copy-start.2 = (f32[1024,512]{1,0:T(8,128)}, f32[1024,512]{1,0:T(8,128)S(1)}, u32[]{:S(2)}) copy-start(f32[1024,512]{1,0:T(8,128)S(1)} %copy.44) | copy-start | bytes 6291460
  83.0 4.9 %copy-start.3 = (s32[1536,2]{0,1:T(2,128)S(1)}, s32[1536,2]{0,1:T(2,128)}, u32[]{:S(2)}) copy-start(s32[1536,2]{0,1:T(2,128)} %param.27) | copy-start | bytes 36868
  83.0 5.0 %copy-start.7 = (s32[1536]{0:T(1024)S(1)}, s32[1536]{0:T(1024)}, u32[]{:S(2)}) copy-start(s32[1536]{0:T(1024)} %param.31) | copy-start | bytes 18436
  83.0 5.0 %copy-start.4 = (f32[1536]{0:T(1024)S(1)}, f32[1536]{0:T(1024)}, u32[]{:S(2)}) copy-start(f32[1536]{0:T(1024)} %param.28) | copy-start | bytes 18436
  83.0 5.0 %copy-start.5 = (f32[1536]{0:T(1024)S(1)}, f32[1536]{0:T(1024)}, u32[]{:S(2)}) copy-start(f32[1536]{0:T(1024)} %param.29) | copy-start | bytes 18436
  83.0 5.0 %copy-start.8 = (f32[1536]{0:T(1024)S(1)}, f32[1536]{0:T(1024)}, u32[]{:S(2)}) copy-start(f32[1536]{0:T(1024)} %param.30) | copy-start | bytes 18436
  83.1 5.9 %collective-permute-start = (f32[1,128,512]{1,2,0:T(8,128)S(1)}, f32[1,128,512]{1,2,0:T(8,128)S(1)}, u32[]{:S(2)}, u32[]{:S(2)}) collective-permute-start(f32[1,128,512]{1,2,0:T(8,128)S(1)} %bitcast_select_fusion.2), channel_id=1, source_target_pairs={{0,8},{8,16},{16,24},{24,32},{32,40},{40,48},{48,56},{56,64},{64,7... | collective-permute-start | bytes 786440 | tf_op jit(solution)/shard_map/ppermute | solution.py:10
  86.6 7.1 %collective-permute-start.1 = (f32[1,128,512]{1,2,0:T(8,128)S(1)}, f32[1,128,512]{1,2,0:T(8,128)S(1)}, u32[]{:S(2)}, u32[]{:S(2)}) collective-permute-start(f32[1,128,512]{1,2,0:T(8,128)S(1)} %bitcast_select_fusion.1), channel_id=1, source_target_pairs={{8,0},{16,8},{24,16},{32,24},{40,32},{48,40},{56,48},{64,56},{72,6... | collective-permute-start | bytes 786440 | tf_op jit(solution)/shard_map/ppermute | solution.py:10
